TPU v7x, 256 devices: a whole 4x4x8 slice. The times are simulated.
256 devices in a mesh: tile: 128 (over x, y, z), rep: 2 (over core).
Axes of the slice: x: 4, y: 4, z: 8, core: 2. Of those that a mesh axis runs over, the one named last changes fastest.
Arguments:
- amplitudes: bfloat16 [2048, 128, 1024], P('tile', None, 'rep'), may hold values from -6 to 6
- integrals: bfloat16 [384, 1024, 1024], P('tile'), may hold values from -0.1875 to 0.1875
- task_cd: int32 [384], P('tile'), may hold values from 0 to 127
- task_ab: int32 [384], P('tile'), may hold values from 0 to 63
- task_allowed: int32 [384], P('tile'), may hold values from 0 to 1, as said below
- mirror: int32 [2048], P(('tile', 'rep')), may hold values from 0 to 2047, as said below
- residual_in: bfloat16 [2048, 64, 1024], P(('tile', 'rep')), may hold values from -6 to 6
Outputs:
- residual_out: bfloat16 [2048, 64, 1024], P(('tile', 'rep'))
Inputs may be any that keep to these rules, and one draw needn't show every extreme that they name: `task_allowed`: in each aligned block of 3 slots (the slots of one device along tile) one to 2 slots are allowed; some block has exactly 2. mirror is an involution on the occupied pairs without fixed points. Split the pairs into aligned blocks of 8; for b < 128, mirror maps block b one to one onto block b + 128.
All inputs are finite; a program needn't handle non-finite values.
Results may differ from a plain program's by a relative error of at most 0.0055.
Values may be sent and summed in bfloat16 or wider, within the bound.
A program may use at most 128 MiB of HBM per device.

v0:
```python
import jax
import jax.numpy as jnp
from jax import lax
from jax.sharding import PartitionSpec as P


def partner_2(shard, axis, bit):
    return lax.ppermute(shard, axis, [(i, i ^ 1 << bit) for i in range(lax.axis_size(axis))])


def per_device(amplitudes, integrals, task_cd, task_ab, task_allowed, mirror, residual_in):
    own_cd, own_ab, own_allowed, integral_tiles = (task_cd, task_ab, task_allowed, integrals)
    every_cd, every_ab, every_allowed = (
        lax.all_gather(own_cd, "tile", axis=0, tiled=True),
        lax.all_gather(own_ab, "tile", axis=0, tiled=True),
        lax.all_gather(own_allowed, "tile", axis=0, tiled=True),
    )
    peer_count = lax.axis_size("tile")
    slot_count = own_cd.shape[0]
    local_rows = residual_in.shape[0]
    tile_width = integral_tiles.shape[1]
    half_cols = amplitudes.shape[2]
    outgoing = jnp.take(amplitudes, every_cd, axis=1).reshape(
        amplitudes.shape[0], peer_count, slot_count, half_cols
    )
    rows_sent = outgoing.shape[0]
    incoming = lax.all_to_all(outgoing, "tile", split_axis=1, concat_axis=0, tiled=True)
    incoming = incoming.reshape(peer_count * rows_sent, slot_count, outgoing.shape[3])
    own_half = lax.dynamic_slice_in_dim(
        integral_tiles, lax.axis_index("rep") * half_cols, half_cols, 2
    )
    products = jnp.einsum(
        "isc,sac->sia", incoming, own_half, preferred_element_type=jnp.float32
    ).astype(jnp.bfloat16)
    products = products.reshape(slot_count, peer_count, rows_sent, tile_width)
    shipped = lax.all_to_all(products, "tile", split_axis=1, concat_axis=0, tiled=True)
    arrived = lax.psum_scatter(
        lax.optimization_barrier(shipped).astype(jnp.float32).astype(jnp.bfloat16),
        "rep",
        scatter_dimension=2,
        tiled=True,
    )
    arrived = arrived.reshape(peer_count * slot_count, local_rows, tile_width)
    tile_ids = jnp.arange(residual_in.shape[1], dtype=jnp.int32)
    weights = ((every_ab[:, None] == tile_ids[None, :]) & (every_allowed[:, None] == 1)).astype(
        jnp.bfloat16
    )
    ladder = jnp.einsum("qa,qrc->rac", weights, arrived, preferred_element_type=jnp.float32)
    summed = residual_in.astype(jnp.float32) + ladder
    partner = partner_2(summed, "tile", peer_count.bit_length() - 2)
    mirrored = jnp.take(partner, mirror % local_rows, axis=0)
    return (0.5 * (summed - mirrored)).astype(jnp.bfloat16)


def solution(mesh):
    return jax.shard_map(
        per_device,
        mesh=mesh,
        in_specs=(
            P("tile", None, "rep"),
            P("tile", None, None),
            P("tile"),
            P("tile"),
            P("tile"),
            P(("tile", "rep")),
            P(("tile", "rep"), None, None),
        ),
        out_specs=P(("tile", "rep"), None, None),
        check_vma=False,
    )
```

profile of v0, /device:TPU:33, one launch (start us, length us, event | category | flops | bytes accessed | tf_op | source)
XLA Modules:
  0.0 635.1 jit_solution(13567470189735164914)
XLA Ops:
  6.5 0.0 copy-start
  6.5 1.4 dynamic-slice
  8.6 0.9 dynamic-update-slice
  9.5 0.8 dynamic-update-slice.1
  10.3 0.8 dynamic-update-slice.2
  11.2 24.7 %all-reduce.3 = (s32[384]{0:T(512)S(1)}, s32[384]{0:T(512)S(1)}, s32[384]{0:T(512)S(1)}) all-reduce(s32[384]{0:T(512)S(1)} %dynamic-update-slice, s32[384]{0:T(512)S(1)} %dynamic-update-slice.1, s32[384]{0:T(512)S(1)} %dynamic-update-slice.2), channel_id=1, replica_groups=mesh['tile'=128,'rep'=2] {'tile'}, use_global_device_ids=true, to_apply=%add | all-reduce | flops 1152 | bytes 9216
  35.9 0.0 copy-done
  35.9 38.9 %gather_fusion = bf16[384,16,512]{2,0,1:T(8,128)(2,1)} fusion(bf16[16,128,512]{2,1,0:T(8,128)(2,1)S(1)} %copy-done, s32[1024]{0:T(1024)S(1)} %pad_clamp_fusion.1), kind=kCustom, calls=%fused_computation | custom fusion | bytes 12584448 | tf_op jit(solution)/shard_map/jit(_take)/gather | solution.py:23
  74.8 9.0 %copy.14 = bf16[16,384,512]{2,0,1:T(8,128)(2,1)} copy(bf16[16,384,512]{2,1,0:T(8,128)(2,1)} %bitcast.43) | data formatting | bytes 12582912 | tf_op jit(solution)/shard_map/jit(_take)/gather | solution.py:23
  83.8 0.2 broadcast_in_dim.29
  84.0 6.8 %broadcast_select_fusion = bf16[16,128,3,512]{3,0,2,1:T(8,128)(2,1)} fusion(bf16[16,128,3,512]{3,0,2,1:T(8,128)(2,1)} %bitcast.42, pred[128,3]{1,0:T(8,128)(4,1)S(1)} %broadcast_in_dim.29), kind=kLoop, calls=%fused_computation.6 | loop fusion | flops 3145728 | bytes 12583296 | tf_op jit(solution)/shard_map/jit(_take)/select_n | solution.py:23
  90.8 7.0 %all-to-all-start = ((bf16[16,128,3,512]{3,0,2,1:T(8,128)(2,1)}), bf16[16,128,3,512]{3,0,2,1:T(8,128)(2,1)}, u32[]{:S(2)}, u32[]{:S(2)}) async-start(bf16[16,128,3,512]{3,0,2,1:T(8,128)(2,1)} %broadcast_select_fusion), calls=%async_computation | async-start | bytes 12582912 | tf_op jit(solution)/shard_map/all_to_all | solution.py:27
  97.8 0.0 reduce-scatter.4.cloned.1.call-start
  97.9 137.1 %all-to-all-done = bf16[16,128,3,512]{3,0,2,1:T(8,128)(2,1)} async-done(((bf16[16,128,3,512]{3,0,2,1:T(8,128)(2,1)}), bf16[16,128,3,512]{3,0,2,1:T(8,128)(2,1)}, u32[]{:S(2)}, u32[]{:S(2)}) %all-to-all-start) | async-done | bytes 6291488 | tf_op jit(solution)/shard_map/all_to_all | solution.py:27
  235.0 3.7 copy.15
  238.7 11.6 %convolution_convert_fusion = bf16[3,2048,1024]{2,1,0:T(8,128)(2,1)} fusion(bf16[2048,3,512]{2,0,1:T(8,128)(2,1)S(1)} %bitcast.45, bf16[3,1024,1024]{2,1,0:T(8,128)(2,1)} %param.8, s32[]{:T(128)S(6)} %select_n.31), kind=kOutput, calls=%fused_computation.2 | convolution fusion | flops 6448742400 | bytes 22020100 | tf_op jit(solution)/shard_map/isc,sac->sia/dot_general | solution.py:32
  250.3 6.2 copy.16
  256.5 275.1 %all_to_all.33 = bf16[3,128,16,1024]{3,2,0,1:T(8,128)(2,1)S(1)} all-to-all(bf16[3,128,16,1024]{3,2,0,1:T(8,128)(2,1)S(1)} %copy.16), channel_id=1, replica_groups=mesh['tile'=128,'rep'=2] {'tile'}, dimensions={1} | all-to-all | bytes 25165824 | tf_op jit(solution)/shard_map/all_to_all | solution.py:36
  531.6 5.2 copy.21
  536.8 0.0 copy-start.3
  536.8 0.0 reduce-scatter.4.cloned.1.call-update
  536.8 0.0 copy-start.4
  536.8 28.6 %reduce-scatter.4.cloned.1.call-done = bf16[8,393216]{1,0:T(8,128)(2,1)} async-done(((bf16[16,393216]{1,0:T(8,128)(2,1)}), bf16[8,393216]{1,0:T(8,128)(2,1)}) %reduce-scatter.4.cloned.1.call-update) | async-done | bytes 6291472
  565.4 0.0 copy-done.3
  565.4 0.0 copy-start.1
  565.4 6.8 %bitcast_add_fusion = f32[8,64,1024]{2,1,0:T(8,128)S(1)} fusion(bf16[8,64,1024]{2,1,0:T(8,128)(2,1)S(1)} %copy-done.3, bf16[1,8,384,1024]{3,1,2,0:T(8,128)(2,1)} %bitcast.46, s32[384]{0:T(512)S(1)} %get-tuple-element.6, pred[384]{0:T(512)(128)(4,1)S(1)} %broadcast_compare_fusion), kind=kOutput, calls=%fused_computation.8 | convolution fusion | flops 403750912 | bytes 9439104 | tf_op jit(solution)/shard_map/qa,qrc->rac/dot_general | solution.py:48
  572.2 0.0 copy-start.2
  572.2 1.3 copy-done.2
  573.5 2.7 collective-permute-start
  576.2 0.0 copy-done.4
  576.2 44.6 %collective-permute-done = f32[8,64,1024]{2,1,0:T(8,128)} collective-permute-done((f32[8,64,1024]{2,1,0:T(8,128)S(1)}, f32[8,64,1024]{2,1,0:T(8,128)}, u32[]{:S(2)}, u32[]{:S(2)}) %collective-permute-start) | collective-permute-done | bytes 2097184 | tf_op jit(solution)/shard_map/ppermute | solution.py:8
  620.9 3.6 gather_fusion.1
  624.5 3.8 multiply_convert_fusion
  628.2 0.0 copy-done.1
  (9 shorter events, 0.1 us)
Async XLA Ops:
  6.5 29.4 %copy-start = (bf16[16,128,512]{2,1,0:T(8,128)(2,1)S(1)}, bf16[16,128,512]{2,1,0:T(8,128)(2,1)}, u32[]{:S(2)}) copy-start(bf16[16,128,512]{2,1,0:T(8,128)(2,1)} %param.7) | copy-start | bytes 6291460
  90.8 144.2 %all-to-all-start = ((bf16[16,128,3,512]{3,0,2,1:T(8,128)(2,1)}), bf16[16,128,3,512]{3,0,2,1:T(8,128)(2,1)}, u32[]{:S(2)}, u32[]{:S(2)}) async-start(bf16[16,128,3,512]{3,0,2,1:T(8,128)(2,1)} %broadcast_select_fusion), calls=%async_computation | async-start | bytes 12582912 | tf_op jit(solution)/shard_map/all_to_all | solution.py:27
  97.8 467.6 %reduce-scatter.4.cloned.1.call-start = ((), (), s32[]{:S(2)}) async-start(), calls=%async_computation.3 | async-start | bytes 18874368
  536.8 28.6 %copy-start.3 = (bf16[8,64,1024]{2,1,0:T(8,128)(2,1)S(1)}, bf16[8,64,1024]{2,1,0:T(8,128)(2,1)}, u32[]{:S(2)}) copy-start(bf16[8,64,1024]{2,1,0:T(8,128)(2,1)} %param.13) | copy-start | bytes 3145732
  536.8 39.4 %copy-start.4 = (s32[8]{0:T(128)S(1)}, s32[8]{0:T(128)}, u32[]{:S(2)}) copy-start(s32[8]{0:T(128)} %param.12) | copy-start | bytes 100
  565.4 62.8 %copy-start.1 = (bf16[16,128,512]{2,1,0:T(8,128)(2,1)S(1)}, bf16[16,128,512]{2,1,0:T(8,128)(2,1)}, u32[]{:S(2)}) copy-start(bf16[16,128,512]{2,1,0:T(8,128)(2,1)} %param.7) | copy-start | bytes 6291460
  572.2 1.4 copy-start.2
  573.5 47.4 %collective-permute-start = (f32[8,64,1024]{2,1,0:T(8,128)S(1)}, f32[8,64,1024]{2,1,0:T(8,128)}, u32[]{:S(2)}, u32[]{:S(2)}) collective-permute-start(f32[8,64,1024]{2,1,0:T(8,128)S(1)} %bitcast_add_fusion), channel_id=1, source_target_pairs={{0,128},{2,130},{4,132},{6,134},{8,136},{10,138},{12,140},{14,142}... | collective-permute-start | bytes 6291464 | tf_op jit(solution)/shard_map/ppermute | solution.py:8
Sparse Core Ops, SparseCore 0:
  536.9 28.4 reduce-scatter.3
where the time goes:
time: 638 us; the launch traced here: 635 us
  blocking collectives  300 us (47%)
  waiting for transfers between devices  210 us (33%)
  local copies, waits for them, and re-layouts  72.1 us (11%)
  matrix products  18.3 us (3%)
  between operations  14.2 us (2%)
  other arithmetic  10.6 us (2%)
  starting transfers between devices  9.77 us (2%)
    all_to_all x1, blocking collectives, per_device(): lax.all_to_all(products, 'tile', split_axis=1, concat_axis=0, tiled=True)  275 us
    all_to_all x1, waiting for transfers between devices, per_device(): lax.all_to_all(outgoing, 'tile', split_axis=1, concat_axis=0, tiled=True)  137 us
    gather x2, local copies, waits for them, and re-layouts, per_device(): jnp.take(amplitudes, every_cd, axis=1)  47.8 us
    ppermute x1, waiting for transfers between devices, partner_2(): lax.ppermute(shard, axis, [(i, i ^ 1 << bit) for i in range(lax.axis_size...  44.6 us
    unnamed x2, waiting for transfers between devices  28.6 us
    unnamed x1, blocking collectives  24.7 us
  transfers between devices with their start and end apart: 3, of which 3 were waited for; matrix products, arithmetic and copies ran while one was open for 0% of the time, Pallas kernels for 0%

commit v1 on v0

v1 whole, which is shorter than its diff:
```python
import jax
import jax.numpy as jnp
from jax import lax
from jax.sharding import PartitionSpec as P

BOTH = ("tile", "rep")


def partner_2(shard, axis, bit):
    return lax.ppermute(shard, axis, [(i, i ^ 1 << bit) for i in range(lax.axis_size(axis))])


def per_device(amplitudes, integrals, task_cd, task_ab, task_allowed, mirror, residual_in):
    peer_count = lax.axis_size("tile")
    rep_count = lax.axis_size("rep")
    rows_own, _, half_cols = amplitudes.shape
    local_rows = residual_in.shape[0]
    tile_width = integrals.shape[1]
    rep = lax.axis_index("rep")

    order = jnp.argsort(1 - task_allowed, stable=True)
    slot = order[rep]
    mine = jnp.stack([task_cd[slot], task_ab[slot], task_allowed[slot]])
    every = lax.all_gather(mine, BOTH, axis=0, tiled=False)
    every_cd, every_ab, every_allowed = every[:, 0], every[:, 1], every[:, 2]

    outgoing = jnp.take(amplitudes, every_cd, axis=1)
    incoming = lax.all_to_all(outgoing, BOTH, split_axis=1, concat_axis=0, tiled=True)
    incoming = incoming.reshape(peer_count, rep_count, rows_own, half_cols)
    integral = lax.dynamic_index_in_dim(integrals, slot, axis=0, keepdims=False)
    integral = integral.reshape(tile_width, rep_count, half_cols)
    halves = jnp.einsum(
        "tric,arc->rtia", incoming, integral, preferred_element_type=jnp.float32
    ).astype(jnp.bfloat16)

    contribution = (halves[0].astype(jnp.float32) + halves[1].astype(jnp.float32)).astype(
        jnp.bfloat16
    )
    contribution = contribution.reshape(peer_count * rep_count, local_rows, tile_width)
    arrived = lax.all_to_all(contribution, BOTH, split_axis=0, concat_axis=0, tiled=True)

    tile_ids = jnp.arange(residual_in.shape[1], dtype=jnp.int32)
    weights = ((every_ab[:, None] == tile_ids[None, :]) & (every_allowed[:, None] == 1)).astype(
        jnp.bfloat16
    )
    ladder = jnp.einsum("qa,qrc->rac", weights, arrived, preferred_element_type=jnp.float32)
    summed = residual_in.astype(jnp.float32) + ladder
    partner = partner_2(summed, "tile", peer_count.bit_length() - 2)
    mirrored = jnp.take(partner, mirror % local_rows, axis=0)
    return (0.5 * (summed - mirrored)).astype(jnp.bfloat16)

def solution(mesh):
    return jax.shard_map(
        per_device,
        mesh=mesh,
        in_specs=(
            P("tile", None, "rep"),
            P("tile", None, None),
            P("tile"),
            P("tile"),
            P("tile"),
            P(("tile", "rep")),
            P(("tile", "rep"), None, None),
        ),
        out_specs=P(("tile", "rep"), None, None),
        check_vma=False,
    )
```

time: 638 us -> 398 us (0.62)
  blocking collectives: 300 us -> 184 us
  waiting for transfers between devices: 210 us -> 139 us
  local copies, waits for them, and re-layouts: 72.1 us -> 38.2 us
  between operations: 14.2 us -> 2.04 us
    all_to_all x1, blocking collectives: 275 us -> 104 us  [per_device(): lax.all_to_all(contribution, BOTH, split_axis=0, concat_axis=0, tiled=True)]
    unnamed x1, blocking collectives: 24.7 us -> 79.6 us
    all_to_all x1, waiting for transfers between devices: 137 us -> 91.1 us  [per_device(): lax.all_to_all(outgoing, BOTH, split_axis=1, concat_axis=0, tiled=True)]
    gather x2 -> x1, local copies, waits for them, and re-layouts: 47.8 us -> 15 us  [per_device(): outgoing = jnp.take(amplitudes, every_cd, axis=1)]
    unnamed x2 -> x0, waiting for transfers between devices: 28.6 us -> none
    dynamic_slice x0 -> x5, local copies, waits for them, and re-layouts: none -> 7.43 us  [the longest x3 3.79 us: per_device(): mine = jnp.stack([task_cd[slot], task_ab[slot], task_allowed[slot]])]
  transfers between devices with their start and end apart: 3 -> 2, of which waited for: 3 -> 2; matrix products, arithmetic and copies ran while one was open for 0% -> 2% of each run, Pallas kernels for 0% -> 0%
where the time goes in v1:
time: 398 us
  blocking collectives  184 us (46%)
  waiting for transfers between devices  139 us (35%)
  local copies, waits for them, and re-layouts  38.2 us (10%)
  matrix products  13.1 us (3%)
  other arithmetic  12.6 us (3%)
  starting transfers between devices  9.08 us (2%)
    all_to_all x1, blocking collectives, per_device(): lax.all_to_all(contribution, BOTH, split_axis=0, concat_axis=0, tiled=True)  104 us
    all_to_all x1, waiting for transfers between devices, per_device(): lax.all_to_all(outgoing, BOTH, split_axis=1, concat_axis=0, tiled=True)  91.1 us
    unnamed x1, blocking collectives  79.6 us
    ppermute x1, waiting for transfers between devices, partner_2(): lax.ppermute(shard, axis, [(i, i ^ 1 << bit) for i in range(lax.axis_size...  48 us
    gather x1, local copies, waits for them, and re-layouts, per_device(): outgoing = jnp.take(amplitudes, every_cd, axis=1)  15 us
    dot_general x1, matrix products, per_device(): jnp.einsum('tric,arc->rtia', incoming, integral, preferred_element_type=j...  10.4 us
    all_to_all x1, starting transfers between devices, per_device(): lax.all_to_all(outgoing, BOTH, split_axis=1, concat_axis=0, tiled=True)  8.83 us
  transfers between devices with their start and end apart: 2, of which 2 were waited for; matrix products, arithmetic and copies ran while one was open for 2% of the time, Pallas kernels for 0%

profile of v1, /device:TPU:33, one launch (start us, length us, event | category | flops | bytes accessed | tf_op | source)
XLA Modules:
  0.0 397.7 jit_solution(9754747565145856149)
XLA Ops:
  0.0 0.0 copy-start
  0.0 0.8 broadcast_subtract_fusion
  0.8 0.7 sort.17
  1.6 0.6 dynamic_slice.16
  4.1 1.2 dynamic_slice.19
  5.3 1.2 dynamic_slice.17
  6.6 1.3 dynamic_slice.18
  7.9 2.1 add_dynamic-update-slice_fusion
  10.0 79.6 %all-reduce = s32[768]{0:T(1024)S(1)} all-reduce(s32[768]{0:T(1024)S(1)} %add_dynamic-update-slice_fusion), channel_id=2, replica_groups=mesh['tile'=128,'rep'=2] {'tile','rep'}, use_global_device_ids=true, to_apply=%add | all-reduce | flops 768 | bytes 6144
  89.5 0.2 reshape.42
  89.7 0.2 slice_reduce_fusion
  90.0 0.2 fusion.5
  90.2 0.0 copy-done
  90.2 15.0 %gather_fusion = bf16[256,16,512]{2,0,1:T(8,128)(2,1)} fusion(bf16[16,128,512]{2,1,0:T(8,128)(2,1)S(1)} %copy-done, s32[1024]{0:T(1024)S(1)} %pad_clamp_fusion.1), kind=kCustom, calls=%fused_computation | custom fusion | bytes 8389632 | tf_op jit(solution)/shard_map/jit(_take)/gather | solution.py:27
  105.2 2.7 select_bitcast_fusion
  107.9 4.4 %copy.14 = bf16[16,256,512]{2,0,1:T(8,128)(2,1)} copy(bf16[16,256,512]{2,1,0:T(8,128)(2,1)S(1)} %select_bitcast_fusion) | data formatting | bytes 8388608 | tf_op jit(solution)/shard_map/jit(_take)/select_n | solution.py:27
  112.2 8.8 %all-to-all-start = ((bf16[16,256,512]{2,0,1:T(8,128)(2,1)}), bf16[16,256,512]{2,0,1:T(8,128)(2,1)}, u32[]{:S(2)}, u32[]{:S(2)}) async-start(bf16[16,256,512]{2,0,1:T(8,128)(2,1)} %copy.14), calls=%async_computation | async-start | bytes 8388608 | tf_op jit(solution)/shard_map/all_to_all | solution.py:28
  121.1 3.1 constant_dynamic-slice_fusion
  124.1 3.9 copy.23
  128.1 91.1 %all-to-all-done = bf16[16,256,512]{2,0,1:T(8,128)(2,1)} async-done(((bf16[16,256,512]{2,0,1:T(8,128)(2,1)}), bf16[16,256,512]{2,0,1:T(8,128)(2,1)}, u32[]{:S(2)}, u32[]{:S(2)}) %all-to-all-start) | async-done | bytes 4194336 | tf_op jit(solution)/shard_map/all_to_all | solution.py:28
  219.2 10.4 %convolution_convert_fusion = bf16[2,128,16,1024]{3,1,2,0:T(8,128)(2,1)S(1)} fusion(bf16[1024,2,512,1]{0,2,3,1:T(8,128)(2,1)} %bitcast.21, bf16[128,2,16,512]{3,2,1,0:T(8,128)(2,1)} %bitcast.4), kind=kOutput, calls=%fused_computation.3 | convolution fusion | flops 4299161600 | bytes 14680064 | tf_op jit(solution)/shard_map/tric,arc->rtia/dot_general | solution.py:32
  229.6 2.1 add_convert_fusion
  231.7 2.3 copy.18
  234.0 0.0 copy-start.2
  234.0 104.1 %all_to_all.20 = bf16[256,8,1024]{2,1,0:T(8,128)(2,1)S(1)} all-to-all(bf16[256,8,1024]{2,1,0:T(8,128)(2,1)S(1)} %bitcast.20), channel_id=1, replica_groups=mesh['tile'=128,'rep'=2] {'tile','rep'}, dimensions={0} | all-to-all | bytes 8388608 | tf_op jit(solution)/shard_map/all_to_all | solution.py:40
  338.1 0.0 copy-done.2
  338.1 0.0 copy-start.3
  338.1 2.6 bitcast_add_fusion
  340.7 0.0 copy-start.1
  340.8 1.4 copy-done.1
  342.1 0.2 collective-permute-start
  342.4 0.0 copy-done.3
  342.4 48.0 %collective-permute-done = f32[8,64,1024]{2,1,0:T(8,128)} collective-permute-done((f32[8,64,1024]{2,1,0:T(8,128)S(1)}, f32[8,64,1024]{2,1,0:T(8,128)}, u32[]{:S(2)}, u32[]{:S(2)}) %collective-permute-start) | collective-permute-done | bytes 2097184 | tf_op jit(solution)/shard_map/ppermute | solution.py:10
  390.3 3.6 gather_fusion.1
  393.9 3.8 multiply_convert_fusion
  (5 shorter events, 0.0 us)
Async XLA Ops:
  0.0 90.2 %copy-start = (bf16[16,128,512]{2,1,0:T(8,128)(2,1)S(1)}, bf16[16,128,512]{2,1,0:T(8,128)(2,1)}, u32[]{:S(2)}) copy-start(bf16[16,128,512]{2,1,0:T(8,128)(2,1)} %param.7) | copy-start | bytes 6291460
  112.2 106.9 %all-to-all-start = ((bf16[16,256,512]{2,0,1:T(8,128)(2,1)}), bf16[16,256,512]{2,0,1:T(8,128)(2,1)}, u32[]{:S(2)}, u32[]{:S(2)}) async-start(bf16[16,256,512]{2,0,1:T(8,128)(2,1)} %copy.14), calls=%async_computation | async-start | bytes 8388608 | tf_op jit(solution)/shard_map/all_to_all | solution.py:28
  234.0 104.1 %copy-start.2 = (bf16[8,64,1024]{2,1,0:T(8,128)(2,1)S(1)}, bf16[8,64,1024]{2,1,0:T(8,128)(2,1)}, u32[]{:S(2)}) copy-start(bf16[8,64,1024]{2,1,0:T(8,128)(2,1)} %param.13) | copy-start | bytes 3145732
  338.1 4.2 %copy-start.3 = (s32[8]{0:T(128)S(1)}, s32[8]{0:T(128)}, u32[]{:S(2)}) copy-start(s32[8]{0:T(128)} %param.12) | copy-start | bytes 100
  340.7 1.4 copy-start.1
  342.1 48.2 %collective-permute-start = (f32[8,64,1024]{2,1,0:T(8,128)S(1)}, f32[8,64,1024]{2,1,0:T(8,128)}, u32[]{:S(2)}, u32[]{:S(2)}) collective-permute-start(f32[8,64,1024]{2,1,0:T(8,128)S(1)} %bitcast_add_fusion), channel_id=1, source_target_pairs={{0,128},{2,130},{4,132},{6,134},{8,136},{10,138},{12,140},{14,142}... | collective-permute-start | bytes 6291464 | tf_op jit(solution)/shard_map/ppermute | solution.py:10
